TPU v7x, 32 devices: a whole 2x2x4 slice. The times are simulated.
32 devices in a mesh: dp: 8 (over y, x, core), tensor: 4 (over z).
Axes of the slice: x: 2, y: 2, z: 4, core: 2. Of those that a mesh axis runs over, the one named last changes fastest.
Arguments:
- frames: bfloat16 [2, 8, 1152, 1024], P(None, 'dp'), may hold values from -6 to 6
- skip_frames: bfloat16 [2, 8, 1152, 1024], P(None, 'dp'), may hold values from -6 to 6
- cotangent: bfloat16 [2, 8, 1152, 1024], P(None, 'dp'), may hold values from -6 to 6
- lengths: int32 [2, 8], P(None, 'dp'), may hold values from 288 to 1152, as said below
- time_steps: int32 [2, 8], P(None, 'dp'), may hold values from 0 to 63
- time_table: bfloat16 [64, 1024], replicated, may hold values from -6 to 6
- w_skip: bfloat16 [2048, 1024], replicated, may hold values from -0.125 to 0.125
- w_gamma_attn: bfloat16 [1024, 1024], replicated, may hold values from -0.1875 to 0.1875
- w_gamma_ffn: bfloat16 [1024, 1024], replicated, may hold values from -0.1875 to 0.1875
- w_qkv: bfloat16 [3, 1024, 1024], P(None, None, 'tensor'), may hold values from -0.1875 to 0.1875
- w_out: bfloat16 [1024, 1024], P('tensor'), may hold values from -0.75 to 0.75
- w_up: bfloat16 [1024, 4096], P(None, 'tensor'), may hold values from -0.1875 to 0.1875
- b_up: bfloat16 [4096], P('tensor'), may hold values from -4 to 4
- w_down: bfloat16 [4096, 1024], P('tensor'), may hold values from -0.09375 to 0.09375
Outputs:
- mixed: bfloat16 [2, 8, 1152, 1024], P(None, 'dp')
- grad_frames: bfloat16 [2, 8, 1152, 1024], P(None, 'dp')
- grad_skip: bfloat16 [2, 8, 1152, 1024], P(None, 'dp')
- grad_table: float32 [64, 1024], P('dp')
- grad_w_skip: float32 [2048, 1024], P(('dp', 'tensor'))
- grad_w_gamma_attn: float32 [1024, 1024], P('dp')
- grad_w_gamma_ffn: float32 [1024, 1024], P('dp')
- grad_w_qkv: float32 [3, 1024, 1024], P(None, 'dp', 'tensor')
- grad_w_out: float32 [1024, 1024], P('tensor', 'dp')
- grad_w_up: float32 [1024, 4096], P('dp', 'tensor')
- grad_b_up: float32 [4096], P('tensor')
- grad_w_down: float32 [4096, 1024], P('tensor', 'dp')
Inputs may be any that keep to these rules, and one draw needn't show every extreme that they name: `lengths`: the live frames of an utterance are its first slots; in every micro-batch one utterance fills all 1152 slots.
All inputs are finite; a program needn't handle non-finite values.
Results may differ from a plain program's by a relative error of at most 0.025.
The roundings to bfloat16 on the way count: a program that leaves them out, or rounds other values in their place, can miss the bound.
Values may be sent and summed in bfloat16 or wider, within the bound.
No kernel may reach another device: no remote copies, remote signals or barrier semaphores. Data moves between devices by JAX's collectives and lax.ppermute only.
A program may use at most 256 MiB of HBM per device.

v0:
```python
import math
import jax
import jax.numpy as jnp
from jax import lax
from jax.sharding import PartitionSpec as P

HD = 64
EPSILON = 1e-06
MASKED = -1e30


def rope_tables(length, head_size):
    half_size = head_size // 2
    places = jnp.arange(length, dtype=jnp.float32)
    frequency = jnp.exp(
        jnp.arange(half_size, dtype=jnp.float32) * (-2.0 * math.log(10000.0) / head_size)
    )
    angles = places[:, None] * frequency[None, :]
    return (jnp.cos(angles)[:, None, :], jnp.sin(angles)[:, None, :])


def rotate(values, cosine, sine):
    half_size = values.shape[-1] // 2
    front_half = values[..., :half_size]
    back_half = values[..., half_size:]
    return jnp.concatenate(
        [front_half * cosine - back_half * sine, back_half * cosine + front_half * sine], axis=-1
    )


def unrotate(gradient, cosine, sine):
    half_size = gradient.shape[-1] // 2
    front_half = gradient[..., :half_size]
    back_half = gradient[..., half_size:]
    return jnp.concatenate(
        [front_half * cosine + back_half * sine, back_half * cosine - front_half * sine], axis=-1
    )


def normalize(hidden):
    factor = lax.rsqrt(jnp.mean(hidden * hidden, axis=-1, keepdims=True) + EPSILON)
    return (hidden * factor, factor)


def norm_back(grad_normed, normed, factor):
    return factor * (grad_normed - normed * jnp.mean(grad_normed * normed, axis=-1, keepdims=True))


def scores_of(queries, keys_rot, live_keys, score_scale):
    raw_scores = (
        jnp.einsum("slhe,smhe->shlm", queries, keys_rot, preferred_element_type=jnp.float32)
        * score_scale
    )
    return jnp.where(live_keys[:, None, None, :], raw_scores, MASKED)


def gelu_exact(values):
    return jax.nn.gelu(values, approximate=False)


def local(
    frames,
    skip_frames,
    cotangent,
    lengths,
    time_steps,
    time_table,
    w_skip,
    w_gamma_attn,
    w_gamma_ffn,
    w_qkv,
    w_out,
    w_up,
    b_up,
    w_down,
):
    micro_count, seq_count, length, model_width = frames.shape
    local_width = w_qkv.shape[2]
    heads_local = local_width // HD
    row_count = seq_count * length
    table_rows = time_table.shape[0]
    score_scale = 1.0 / math.sqrt(HD)
    cosine, sine = rope_tables(length, HD)
    places = jnp.arange(length)
    bias_f32 = b_up.astype(jnp.float32)
    grad_w_down = jnp.zeros(w_down.shape, jnp.float32)
    grad_w_up = jnp.zeros(w_up.shape, jnp.float32)
    grad_b_up = jnp.zeros(b_up.shape, jnp.float32)
    grad_w_out = jnp.zeros(w_out.shape, jnp.float32)
    grad_w_qkv = jnp.zeros(w_qkv.shape, jnp.float32)
    grad_w_skip = jnp.zeros(w_skip.shape, jnp.float32)
    grad_gamma_attn = jnp.zeros(w_gamma_attn.shape, jnp.float32)
    grad_gamma_ffn = jnp.zeros(w_gamma_ffn.shape, jnp.float32)
    grad_table = jnp.zeros(time_table.shape, jnp.float32)
    mixed_list = []
    frame_grads = []
    skip_grads_list = []
    for micro_index in range(micro_count):
        live_keys = places[None, :] < lengths[micro_index][:, None]
        live_rows = live_keys.astype(jnp.float32)[:, :, None]
        onehot = time_steps[micro_index][:, None] == jnp.arange(table_rows)[None, :]
        condition = jnp.dot(
            onehot.astype(jnp.bfloat16), time_table, preferred_element_type=jnp.float32
        ).astype(jnp.bfloat16)
        gain_attn = 1.0 + jnp.dot(condition, w_gamma_attn, preferred_element_type=jnp.float32)
        gain_ffn = 1.0 + jnp.dot(condition, w_gamma_ffn, preferred_element_type=jnp.float32)
        joined = jnp.concatenate([frames[micro_index], skip_frames[micro_index]], axis=-1).reshape(
            row_count, 2 * model_width
        )
        skip_mixed = jnp.dot(joined, w_skip, preferred_element_type=jnp.float32).reshape(
            seq_count, length, model_width
        )
        normed_one, factor_one = normalize(skip_mixed)
        attn_in = (
            (normed_one * gain_attn[:, None, :])
            .astype(jnp.bfloat16)
            .reshape(row_count, model_width)
        )
        projected = jnp.einsum("rd,cde->cre", attn_in, w_qkv, preferred_element_type=jnp.float32)
        projected = projected.reshape(3, seq_count, length, heads_local, HD)
        queries = rotate(projected[0], cosine, sine).astype(jnp.bfloat16)
        keys_rot = rotate(projected[1], cosine, sine).astype(jnp.bfloat16)
        values = projected[2].astype(jnp.bfloat16)
        raw_scores = scores_of(queries, keys_rot, live_keys, score_scale)
        maxima = jnp.max(raw_scores, axis=-1, keepdims=True)
        logsum = maxima + jnp.log(jnp.sum(jnp.exp(raw_scores - maxima), axis=-1, keepdims=True))
        weights_low = jnp.exp(raw_scores - logsum).astype(jnp.bfloat16)
        context = jnp.einsum(
            "shlm,smhe->slhe", weights_low, values, preferred_element_type=jnp.float32
        ).astype(jnp.bfloat16)
        context = context.reshape(row_count, local_width)
        attn_total = lax.psum(
            jnp.dot(context, w_out, preferred_element_type=jnp.float32).astype(jnp.bfloat16),
            "tensor",
        ).astype(jnp.float32)
        middle = skip_mixed + attn_total.reshape(seq_count, length, model_width)
        normed_two, factor_two = normalize(middle)
        ffn_in = (
            (normed_two * gain_ffn[:, None, :]).astype(jnp.bfloat16).reshape(row_count, model_width)
        )
        pre_act = jnp.dot(ffn_in, w_up, preferred_element_type=jnp.float32) + bias_f32[None, :]
        activated = gelu_exact(pre_act).astype(jnp.bfloat16)
        ffn_total = lax.psum(
            jnp.dot(activated, w_down, preferred_element_type=jnp.float32).astype(jnp.bfloat16),
            "tensor",
        ).astype(jnp.float32)
        result = (middle + ffn_total.reshape(seq_count, length, model_width)) * live_rows
        mixed_list.append(result.astype(jnp.bfloat16))
        grad_low = (cotangent[micro_index] * live_rows.astype(jnp.bfloat16)).reshape(
            row_count, model_width
        )
        grad_out = grad_low.astype(jnp.float32).reshape(seq_count, length, model_width)
        grad_w_down = grad_w_down + jnp.dot(
            activated.T, grad_low, preferred_element_type=jnp.float32
        )
        grad_act = jnp.dot(grad_low, w_down.T, preferred_element_type=jnp.float32)
        _, gelu_back = jax.vjp(gelu_exact, pre_act)
        grad_pre = gelu_back(grad_act)[0].astype(jnp.bfloat16)
        grad_b_up = grad_b_up + jnp.sum(grad_pre.astype(jnp.float32), axis=0)
        grad_w_up = grad_w_up + jnp.dot(ffn_in.T, grad_pre, preferred_element_type=jnp.float32)
        grad_ffn_in = lax.psum(
            jnp.dot(grad_pre, w_up.T, preferred_element_type=jnp.float32).astype(jnp.bfloat16),
            "tensor",
        ).astype(jnp.float32)
        grad_ffn_in = grad_ffn_in.reshape(seq_count, length, model_width)
        gain_ffn_low = jnp.sum(grad_ffn_in * normed_two, axis=1).astype(jnp.bfloat16)
        grad_middle = grad_out + norm_back(
            grad_ffn_in * gain_ffn[:, None, :], normed_two, factor_two
        )
        grad_attn = grad_middle.astype(jnp.bfloat16).reshape(row_count, model_width)
        grad_w_out = grad_w_out + jnp.dot(context.T, grad_attn, preferred_element_type=jnp.float32)
        grad_context = jnp.dot(grad_attn, w_out.T, preferred_element_type=jnp.float32).astype(
            jnp.bfloat16
        )
        grad_context = grad_context.reshape(seq_count, length, heads_local, HD)
        grad_values = jnp.einsum(
            "shlm,slhe->smhe", weights_low, grad_context, preferred_element_type=jnp.float32
        ).astype(jnp.bfloat16)
        grad_probs = jnp.einsum(
            "slhe,smhe->shlm", grad_context, values, preferred_element_type=jnp.float32
        )
        probs = jnp.exp(scores_of(queries, keys_rot, live_keys, score_scale) - logsum)
        inner_sum = jnp.sum(probs * grad_probs, axis=-1, keepdims=True)
        grad_scores = (probs * (grad_probs - inner_sum)).astype(jnp.bfloat16)
        grad_queries = (
            jnp.einsum("shlm,smhe->slhe", grad_scores, keys_rot, preferred_element_type=jnp.float32)
            * score_scale
        )
        grad_keys = (
            jnp.einsum("shlm,slhe->smhe", grad_scores, queries, preferred_element_type=jnp.float32)
            * score_scale
        )
        grad_proj = jnp.stack(
            [
                unrotate(grad_queries, cosine, sine).astype(jnp.bfloat16),
                unrotate(grad_keys, cosine, sine).astype(jnp.bfloat16),
                grad_values,
            ]
        ).reshape(3, row_count, local_width)
        grad_w_qkv = grad_w_qkv + jnp.einsum(
            "rd,cre->cde", attn_in, grad_proj, preferred_element_type=jnp.float32
        )
        grad_attn_in = lax.psum(
            jnp.einsum("cre,cde->rd", grad_proj, w_qkv, preferred_element_type=jnp.float32).astype(
                jnp.bfloat16
            ),
            "tensor",
        ).astype(jnp.float32)
        grad_attn_in = grad_attn_in.reshape(seq_count, length, model_width)
        gain_attn_low = jnp.sum(grad_attn_in * normed_one, axis=1).astype(jnp.bfloat16)
        grad_base = grad_middle + norm_back(
            grad_attn_in * gain_attn[:, None, :], normed_one, factor_one
        )
        grad_base = grad_base.astype(jnp.bfloat16).reshape(row_count, model_width)
        grad_joined = jnp.dot(grad_base, w_skip.T, preferred_element_type=jnp.float32).reshape(
            seq_count, length, 2 * model_width
        )
        frame_grads.append(grad_joined[..., :model_width].astype(jnp.bfloat16))
        skip_grads_list.append(grad_joined[..., model_width:].astype(jnp.bfloat16))
        grad_w_skip = grad_w_skip + jnp.dot(joined.T, grad_base, preferred_element_type=jnp.float32)
        grad_gamma_attn = grad_gamma_attn + jnp.dot(
            condition.T, gain_attn_low, preferred_element_type=jnp.float32
        )
        grad_gamma_ffn = grad_gamma_ffn + jnp.dot(
            condition.T, gain_ffn_low, preferred_element_type=jnp.float32
        )
        grad_condition = jnp.dot(
            gain_attn_low, w_gamma_attn.T, preferred_element_type=jnp.float32
        ) + jnp.dot(gain_ffn_low, w_gamma_ffn.T, preferred_element_type=jnp.float32)
        grad_table = grad_table + jnp.dot(
            onehot.astype(jnp.float32).T, grad_condition, precision=lax.Precision.HIGHEST
        )
    bias_grad = lax.psum(grad_b_up, "dp")
    summed = (
        lax.psum_scatter(
            grad_w_qkv.astype(jnp.bfloat16), "dp", scatter_dimension=1, tiled=True
        ).astype(jnp.float32),
        lax.psum_scatter(
            grad_w_out.astype(jnp.bfloat16), "dp", scatter_dimension=1, tiled=True
        ).astype(jnp.float32),
        lax.psum_scatter(
            grad_w_up.astype(jnp.bfloat16), "dp", scatter_dimension=0, tiled=True
        ).astype(jnp.float32),
        lax.psum_scatter(
            grad_w_down.astype(jnp.bfloat16), "dp", scatter_dimension=1, tiled=True
        ).astype(jnp.float32),
        lax.psum_scatter(
            grad_gamma_attn.astype(jnp.bfloat16), "dp", scatter_dimension=0, tiled=True
        ).astype(jnp.float32),
        lax.psum_scatter(
            grad_gamma_ffn.astype(jnp.bfloat16), "dp", scatter_dimension=0, tiled=True
        ).astype(jnp.float32),
        lax.psum_scatter(
            grad_table.astype(jnp.bfloat16), "dp", scatter_dimension=0, tiled=True
        ).astype(jnp.float32),
        lax.psum_scatter(
            grad_w_skip.astype(jnp.bfloat16), "dp", scatter_dimension=0, tiled=True
        ).astype(jnp.float32),
    )
    share_rows = summed[7].shape[0] // lax.axis_size("tensor")
    skip_total = lax.dynamic_slice_in_dim(
        summed[7], lax.axis_index("tensor") * share_rows, share_rows, 0
    )
    return (
        jnp.stack(mixed_list),
        jnp.stack(frame_grads),
        jnp.stack(skip_grads_list),
        summed[6],
        skip_total,
        summed[4],
        summed[5],
        summed[0],
        summed[1],
        summed[2],
        bias_grad,
        summed[3],
    )


def solution(mesh):
    placed = (
        P(None, "dp", None, None),
        P(None, "dp", None, None),
        P(None, "dp", None, None),
        P(None, "dp"),
        P(None, "dp"),
        P(),
        P(),
        P(),
        P(),
        P(None, None, "tensor"),
        P("tensor", None),
        P(None, "tensor"),
        P("tensor"),
        P("tensor", None),
    )
    return jax.shard_map(
        local,
        mesh=mesh,
        in_specs=placed,
        out_specs=(
            P(None, "dp", None, None),
            P(None, "dp", None, None),
            P(None, "dp", None, None),
            P("dp", None),
            P(("dp", "tensor"), None),
            P("dp", None),
            P("dp", None),
            P(None, "dp", "tensor"),
            P("tensor", "dp"),
            P("dp", "tensor"),
            P("tensor"),
            P("tensor", "dp"),
        ),
        check_vma=False,
    )
```

profile of v0, /device:TPU:0, one launch (start us, length us, event | category | flops | bytes accessed | tf_op | source)
XLA Modules:
  0.0 1307.0 jit_solution(4355509511752099064)
XLA Ops:
  47.1 12.8 exponential_reduce_fusion
  71.2 10.5 fusion.65
  84.0 10.5 fusion.59
  113.9 158.6 %all-reduce.11.cloned.1.call-done = (bf16[1152,1024]{0,1:T(8,128)(2,1)}, bf16[1152,1024]{0,1:T(8,128)(2,1)}) async-done(((bf16[1152,1024]{0,1:T(8,128)(2,1)}, bf16[1152,1024]{0,1:T(8,128)(2,1)}), (bf16[1152,1024]{0,1:T(8,128)(2,1)}, bf16[1152,1024]{0,1:T(8,128)(2,1)})) %all-reduce.11.cloned.1.call-update) | async-done | bytes 4718608 | tf_op jit(solution)/shard_map/psum | solution.py:132
  278.5 14.3 %multiply_convert_fusion.3 = (bf16[1152,1024]{1,0:T(8,128)(2,1)}, f32[1152,1024]{1,0:T(8,128)S(1)}, f32[1152,1024]{1,0:T(8,128)S(1)}) fusion(f32[1024]{0:T(1024)S(1)} %convert_element_type.428, bf16[1024,1024]{1,0:T(8,128)(2,1)S(1)} %copy-done, f32[1152,1024]{0,1:T(8,128)S(1)} %get-tuple-element.63, f32[1024]{0:T(1024)S(1)} %get-tuple-element.142, ...), kind=kOutput, calls=%fused_computation.69 | convolution fusion | flops 2497314816 | bytes 18625024 | tf_op jit(solution)/shard_map/dot_general | solution.py:141
  302.1 14.4 %multiply_convert_fusion.7 = (bf16[1152,1024]{1,0:T(8,128)(2,1)}, f32[1152,1024]{1,0:T(8,128)S(1)}, f32[1152,1024]{1,0:T(8,128)S(1)}) fusion(f32[1024]{0:T(1024)S(1)} %convert_element_type.428, bf16[1024,1024]{1,0:T(8,128)(2,1)S(1)} %copy-done, f32[1152,1024]{0,1:T(8,128)S(1)} %get-tuple-element.59, f32[1024]{0:T(1024)S(1)} %broadcast_add_fusion.2, ...), kind=kOutput, calls=%fused_computation.88 | convolution fusion | flops 2497314816 | bytes 18625024 | tf_op jit(solution)/shard_map/dot_general | solution.py:141
  339.2 159.1 %all-reduce.9.cloned.1.call-done = (bf16[1152,1024]{0,1:T(8,128)(2,1)}, bf16[1152,1024]{0,1:T(8,128)(2,1)}) async-done(((bf16[1152,1024]{0,1:T(8,128)(2,1)}, bf16[1152,1024]{0,1:T(8,128)(2,1)}), (bf16[1152,1024]{0,1:T(8,128)(2,1)}, bf16[1152,1024]{0,1:T(8,128)(2,1)})) %all-reduce.9.cloned.1.call-update) | async-done | bytes 4718608 | tf_op jit(solution)/shard_map/psum | solution.py:161
  509.6 11.3 fusion.62
  520.9 13.3 %multiply_reduce_fusion.1 = (f32[4,1152]{1,0:T(4,128)S(1)}, f32[4,1152,1152]{1,2,0:T(8,128)}) fusion(f32[4,1152,1152]{1,2,0:T(8,128)} %copy-done.3, f32[4,1152]{1,0:T(4,128)S(1)} %copy-done.67, bf16[1152,4,64]{0,2,1:T(8,128)(2,1)S(1)} %bitcast.283, bf16[1152,4,64]{0,2,1:T(8,128)(2,1)S(1)} %bitcast.274), kind=kOutput, calls=%fused_computation.7 | convolution fusion | flops 695397888 | bytes 43683840 | tf_op jit(solution)/shard_map/slhe,smhe->shlm/dot_general | solution.py:179
  534.2 14.4 %multiply_convert_fusion.1 = bf16[4,1152,1152]{1,2,0:T(8,128)(2,1)S(1)} fusion(f32[4,1152,1152]{1,2,0:T(8,128)} %get-tuple-element.129, f32[4,1152,1152]{1,2,0:T(8,128)} %copy-done.3, f32[4,1152]{1,0:T(4,128)S(1)} %get-tuple-element.128, f32[4,1152]{1,0:T(4,128)S(1)} %copy-done.67), kind=kLoop, calls=%fused_computation.6 | loop fusion | flops 21233664 | bytes 53121024 | tf_op jit(solution)/shard_map/convert_element_type | solution.py:184
  559.4 11.4 fusion.68
  570.8 13.4 %multiply_reduce_fusion = (f32[4,1152]{1,0:T(4,128)S(1)}, f32[4,1152,1152]{1,2,0:T(8,128)}) fusion(f32[4,1152,1152]{1,2,0:T(8,128)} %copy-done.2, f32[4,1152]{1,0:T(4,128)S(1)} %copy-done.65, bf16[1152,4,64]{0,2,1:T(8,128)(2,1)S(1)} %bitcast.285, bf16[1152,4,64]{0,2,1:T(8,128)(2,1)S(1)} %bitcast.276), kind=kOutput, calls=%fused_computation.5 | convolution fusion | flops 695397888 | bytes 43683840 | tf_op jit(solution)/shard_map/slhe,smhe->shlm/dot_general | solution.py:179
  584.2 14.4 %multiply_convert_fusion = bf16[4,1152,1152]{1,2,0:T(8,128)(2,1)S(1)} fusion(f32[4,1152,1152]{1,2,0:T(8,128)} %get-tuple-element.131, f32[4,1152,1152]{1,2,0:T(8,128)} %copy-done.2, f32[4,1152]{1,0:T(4,128)S(1)} %get-tuple-element.130, f32[4,1152]{1,0:T(4,128)S(1)} %copy-done.65), kind=kLoop, calls=%fused_computation.4 | loop fusion | flops 21233664 | bytes 53121024 | tf_op jit(solution)/shard_map/convert_element_type | solution.py:184
  679.3 271.8 %all-reduce.7.cloned.1.call-done = (bf16[1152,1024]{0,1:T(8,128)(2,1)}, bf16[1152,1024]{0,1:T(8,128)(2,1)}, bf16[1152,1024]{0,1:T(8,128)(2,1)}, bf16[1152,1024]{0,1:T(8,128)(2,1)}) async-done(((bf16[1152,1024]{0,1:T(8,128)(2,1)}, bf16[1152,1024]{0,1:T(8,128)(2,1)}, bf16[1152,1024]{0,1:T(8,128)(2,1)}, bf16[1152,1024]{0,1:T(8,128)(2,1)}), (bf16[1152,1024]{0,1:T(8,128)(2,1)}, bf16[1152,1024]{0,1:T(8,128)(2,1)}, ...) | async-done | bytes 9437200 | tf_op jit(solution)/shard_map/psum | solution.py:143
  966.2 9.5 fusion.24
  975.7 8.2 fusion.45
  984.0 9.8 fusion.17
  1003.9 14.4 %psum.71 = f32[1024]{0:T(1024)} all-reduce(f32[1024]{0:T(1024)S(1)} %add.246), channel_id=1, replica_groups=mesh['dp'=8,'tensor'=4] {'dp'}, use_global_device_ids=true, to_apply=%region_35.36 | all-reduce | flops 1024 | bytes 8192 | tf_op jit(solution)/shard_map/psum | solution.py:233
  1020.3 18.4 %reduce-scatter.23.cloned.1.call-done = bf16[128,1024]{1,0:T(8,128)(2,1)} async-done(((bf16[1024,1024]{1,0:T(8,128)(2,1)}), bf16[128,1024]{1,0:T(8,128)(2,1)}) %reduce-scatter.23.cloned.1.call-update) | async-done | bytes 262160 | tf_op jit(solution)/shard_map/reduce_scatter | solution.py:241
  1040.4 35.9 %reduce-scatter.27.cloned.1.call-done = bf16[128,256]{1,0:T(8,128)(2,1)} async-done(((bf16[1024,256]{1,0:T(8,128)(2,1)}), bf16[128,256]{1,0:T(8,128)(2,1)}) %reduce-scatter.27.cloned.1.call-update) | async-done | bytes 65552
  1078.0 40.0 %reduce-scatter.25.cloned.1.call-done = bf16[128,768]{1,0:T(8,128)(2,1)} async-done(((bf16[1024,768]{1,0:T(8,128)(2,1)}), bf16[128,768]{1,0:T(8,128)(2,1)}) %reduce-scatter.25.cloned.1.call-update) | async-done | bytes 196624
  1156.5 43.1 %reduce-scatter.19.cloned.1.call-done = bf16[128,1024]{1,0:T(8,128)(2,1)} async-done(((bf16[1024,1024]{1,0:T(8,128)(2,1)}), bf16[128,1024]{1,0:T(8,128)(2,1)}) %reduce-scatter.19.cloned.1.call-update) | async-done | bytes 262160 | tf_op jit(solution)/shard_map/reduce_scatter | solution.py:247
  1201.4 42.5 %reduce-scatter.21.cloned.1.call-done = bf16[128,1024]{1,0:T(8,128)(2,1)} async-done(((bf16[1024,1024]{1,0:T(8,128)(2,1)}), bf16[128,1024]{1,0:T(8,128)(2,1)}) %reduce-scatter.21.cloned.1.call-update) | async-done | bytes 262160 | tf_op jit(solution)/shard_map/reduce_scatter | solution.py:250
  1245.6 52.7 %reduce-scatter.17.cloned.1.call-done = bf16[256,1024]{1,0:T(8,128)(2,1)} async-done(((bf16[2048,1024]{1,0:T(8,128)(2,1)}), bf16[256,1024]{1,0:T(8,128)(2,1)}) %reduce-scatter.17.cloned.1.call-update) | async-done | bytes 524304 | tf_op jit(solution)/shard_map/reduce_scatter | solution.py:256
  (388 shorter events, 286.4 us)
Async XLA Ops:
  7.2 271.3 %copy-start = (bf16[1024,1024]{1,0:T(8,128)(2,1)S(1)}, bf16[1024,1024]{1,0:T(8,128)(2,1)}, u32[]{:S(2)}) copy-start(bf16[1024,1024]{1,0:T(8,128)(2,1)} %param.25) | copy-start | bytes 6291460
  7.2 265.3 %all-reduce.11.cloned.1.call-start = ((), (), s32[]{:S(2)}) async-start(), calls=%async_computation.18 | async-start | bytes 9437184 | tf_op jit(solution)/shard_map/psum | solution.py:132
  26.4 57.7 %copy-start.26 = (bf16[1,1152,256]{1,2,0:T(8,128)(2,1)}, bf16[1,1152,256]{1,2,0:T(8,128)(2,1)S(1)}, u32[]{:S(2)}) copy-start(bf16[1,1152,256]{1,2,0:T(8,128)(2,1)S(1)} %slice.289) | copy-start | bytes 1769476
  38.6 32.5 %copy-start.28 = (bf16[1,1152,256]{1,2,0:T(8,128)(2,1)}, bf16[1,1152,256]{1,2,0:T(8,128)(2,1)S(1)}, u32[]{:S(2)}) copy-start(bf16[1,1152,256]{1,2,0:T(8,128)(2,1)S(1)} %slice.288) | copy-start | bytes 1769476
  43.0 16.9 %copy-start.38 = (bf16[1152,4,32]{0,2,1:T(8,128)(2,1)}, bf16[1152,4,32]{0,2,1:T(8,128)(2,1)S(1)}, u32[]{:S(2)}) copy-start(bf16[1152,4,32]{0,2,1:T(8,128)(2,1)S(1)} %get-tuple-element.104) | copy-start | bytes 884740
  43.0 16.9 %copy-start.40 = (bf16[1152,4,32]{0,2,1:T(8,128)(2,1)}, bf16[1152,4,32]{0,2,1:T(8,128)(2,1)S(1)}, u32[]{:S(2)}) copy-start(bf16[1152,4,32]{0,2,1:T(8,128)(2,1)S(1)} %get-tuple-element.105) | copy-start | bytes 884740
  43.0 16.9 %copy-start.42 = (bf16[1152,4,32]{0,2,1:T(8,128)(2,1)}, bf16[1152,4,32]{0,2,1:T(8,128)(2,1)S(1)}, u32[]{:S(2)}) copy-start(bf16[1152,4,32]{0,2,1:T(8,128)(2,1)S(1)} %get-tuple-element.108) | copy-start | bytes 884740
  43.0 16.9 %copy-start.44 = (bf16[1152,4,32]{0,2,1:T(8,128)(2,1)}, bf16[1152,4,32]{0,2,1:T(8,128)(2,1)S(1)}, u32[]{:S(2)}) copy-start(bf16[1152,4,32]{0,2,1:T(8,128)(2,1)S(1)} %get-tuple-element.109) | copy-start | bytes 884740
  97.7 400.6 %all-reduce.9.cloned.1.call-start = ((), (), s32[]{:S(2)}) async-start(), calls=%async_computation.17 | async-start | bytes 9437184 | tf_op jit(solution)/shard_map/psum | solution.py:161
  111.9 164.6 %slice-start.2 = ((s8[4718592]{0:T(1024)(128)(4,1)}), s8[524288]{0:T(1024)(128)(4,1)S(1)}, s32[]{:S(2)}) async-start(s8[4718592]{0:T(1024)(128)(4,1)} %bitcast.265), calls=%async_computation.21 | async-start | bytes 1048576
  276.5 25.6 %copy-start.5 = (f32[1152,1024]{0,1:T(8,128)}, f32[1152,1024]{0,1:T(8,128)S(1)}, u32[]{:S(2)}) copy-start(f32[1152,1024]{0,1:T(8,128)S(1)} %get-tuple-element.59) | copy-start | bytes 14155780
  302.1 14.4 %copy-start.90 = (bf16[1152]{0:T(1024)(128)(2,1)S(1)}, bf16[1152]{0:T(1024)(128)(2,1)}, u32[]{:S(2)}) copy-start(bf16[1152]{0:T(1024)(128)(2,1)} %get-tuple-element.139) | copy-start | bytes 6916
  327.2 623.9 %all-reduce.7.cloned.1.call-start = ((), (), s32[]{:S(2)}) async-start(), calls=%async_computation.16 | async-start | bytes 18874368 | tf_op jit(solution)/shard_map/psum | solution.py:143
  534.2 14.4 %copy-start.43 = (bf16[1152,4,32]{0,2,1:T(8,128)(2,1)S(1)}, bf16[1152,4,32]{0,2,1:T(8,128)(2,1)}, u32[]{:S(2)}) copy-start(bf16[1152,4,32]{0,2,1:T(8,128)(2,1)} %copy-done.42) | copy-start | bytes 884740
  534.2 14.4 %copy-start.45 = (bf16[1152,4,32]{0,2,1:T(8,128)(2,1)S(1)}, bf16[1152,4,32]{0,2,1:T(8,128)(2,1)}, u32[]{:S(2)}) copy-start(bf16[1152,4,32]{0,2,1:T(8,128)(2,1)} %copy-done.44) | copy-start | bytes 884740
  627.3 391.0 %reduce-scatter.29.cloned.1.call-start = ((), (), s32[]{:S(2)}) async-start(), calls=%async_computation.15 | async-start | bytes 2359296
  639.1 399.6 %reduce-scatter.23.cloned.1.call-start = ((), (), s32[]{:S(2)}) async-start(), calls=%async_computation.12 | async-start | bytes 2359296 | tf_op jit(solution)/shard_map/reduce_scatter | solution.py:241
  651.7 424.6 %reduce-scatter.27.cloned.1.call-start = ((), (), s32[]{:S(2)}) async-start(), calls=%async_computation.14 | async-start | bytes 589824
  659.3 458.7 %reduce-scatter.25.cloned.1.call-start = ((), (), s32[]{:S(2)}) async-start(), calls=%async_computation.13 | async-start | bytes 1769472
  677.9 477.2 %reduce-scatter.15.cloned.1.call-start = ((), (), s32[]{:S(2)}) async-start(), calls=%async_computation.8 | async-start | bytes 147456 | tf_op jit(solution)/shard_map/reduce_scatter | solution.py:253
  961.8 237.8 %reduce-scatter.19.cloned.1.call-start = ((), (), s32[]{:S(2)}) async-start(), calls=%async_computation.10 | async-start | bytes 2359296 | tf_op jit(solution)/shard_map/reduce_scatter | solution.py:247
  964.6 279.3 %reduce-scatter.21.cloned.1.call-start = ((), (), s32[]{:S(2)}) async-start(), calls=%async_computation.11 | async-start | bytes 2359296 | tf_op jit(solution)/shard_map/reduce_scatter | solution.py:250
  983.9 314.5 %reduce-scatter.17.cloned.1.call-start = ((), (), s32[]{:S(2)}) async-start(), calls=%async_computation.9 | async-start | bytes 4718592 | tf_op jit(solution)/shard_map/reduce_scatter | solution.py:256
  1150.9 149.2 %copy-start.1 = (bf16[1024,1024]{1,0:T(8,128)(2,1)S(1)}, bf16[1024,1024]{1,0:T(8,128)(2,1)}, u32[]{:S(2)}) copy-start(bf16[1024,1024]{1,0:T(8,128)(2,1)} %param.25) | copy-start | bytes 6291460
  (101 other events, 606.3 us)
Sparse Core Ops, SparseCore 0:
  97.8 174.6 all-reduce.10
  327.3 170.9 all-reduce.8
  627.4 323.6 all-reduce.6
  954.2 40.0 reduce-scatter.28
  997.5 41.1 reduce-scatter.22
  1042.2 34.1 reduce-scatter.26
  1079.6 38.3 reduce-scatter.24
  1121.5 33.5 reduce-scatter.14
  1158.5 41.0 reduce-scatter.18
  1202.7 41.0 reduce-scatter.20
  1247.2 51.1 reduce-scatter.16
where the time goes:
time: 1320 us; the launch traced here: 1310 us
  waiting for transfers between devices  824 us (62%)
  matrix products  257 us (19%)
  other arithmetic  124 us (9%)
  local copies, waits for them, and re-layouts  70.4 us (5%)
  between operations  16 us (1%)
  blocking collectives  14.4 us (1%)
    psum x1, waiting for transfers between devices, local(): lax.psum(jnp.dot(activated, w_down, preferred_element_type=jnp.float32).a...  272 us
    psum x1, waiting for transfers between devices, local(): lax.psum(jnp.dot(grad_pre, w_up.T, preferred_element_type=jnp.float32).as...  159 us
    psum x1, waiting for transfers between devices, local(): lax.psum(jnp.dot(context, w_out, preferred_element_type=jnp.float32).asty...  159 us
    unnamed x14, waiting for transfers between devices  76.1 us
    reduce_scatter x1, waiting for transfers between devices, local(): lax.psum_scatter(grad_w_skip.astype(jnp.bfloat16), 'dp', scatter_dimensio...  52.7 us
    unnamed x240, local copies, waits for them, and re-layouts  49.6 us
    reduce_scatter x1, waiting for transfers between devices, local(): lax.psum_scatter(grad_gamma_attn.astype(jnp.bfloat16), 'dp', scatter_dime...  43.1 us
    reduce_scatter x1, waiting for transfers between devices, local(): lax.psum_scatter(grad_gamma_ffn.astype(jnp.bfloat16), 'dp', scatter_dimen...  42.5 us
  transfers between devices with their start and end apart: 11, of which 10 were waited for; matrix products, arithmetic and copies ran while one was open for 13% of the time, Pallas kernels for 0%

commit v1 on v0

--- a/solution.py
+++ b/solution.py
@@ -7,6 +7,11 @@
 HD = 64
 EPSILON = 1e-06
 MASKED = -1e30
+
+
+def meet_goods(payload):
+    part_now = jnp.sum(jax.lax.all_gather(payload, "tensor"), axis=0)
+    return part_now
 
 
 def rope_tables(length, head_size):
@@ -158,9 +163,8 @@
         grad_pre = gelu_back(grad_act)[0].astype(jnp.bfloat16)
         grad_b_up = grad_b_up + jnp.sum(grad_pre.astype(jnp.float32), axis=0)
         grad_w_up = grad_w_up + jnp.dot(ffn_in.T, grad_pre, preferred_element_type=jnp.float32)
-        grad_ffn_in = lax.psum(
-            jnp.dot(grad_pre, w_up.T, preferred_element_type=jnp.float32).astype(jnp.bfloat16),
-            "tensor",
+        grad_ffn_in = meet_goods(
+            jnp.dot(grad_pre, w_up.T, preferred_element_type=jnp.float32).astype(jnp.bfloat16)
         ).astype(jnp.float32)
         grad_ffn_in = grad_ffn_in.reshape(seq_count, length, model_width)
         gain_ffn_low = jnp.sum(grad_ffn_in * normed_two, axis=1).astype(jnp.bfloat16)

time: 1320 us -> 1410 us (1.068)
  waiting for transfers between devices: 824 us -> 885 us
  other arithmetic: 124 us -> 141 us
    all_gather x0 -> x2, waiting for transfers between devices: none -> 216 us  [meet_goods(): part_now = jnp.sum(jax.lax.all_gather(payload, 'tensor'), axis=0)]
    psum x1 -> x0, waiting for transfers between devices: 159 us -> none  [local(): lax.psum(jnp.dot(grad_pre, w_up.T, preferred_element_type=jnp.float32).as...]
    reduce_sum x0 -> x2, other arithmetic: none -> 16.4 us  [meet_goods(): part_now = jnp.sum(jax.lax.all_gather(payload, 'tensor'), axis=0)]
    unnamed x240 -> x232, local copies, waits for them, and re-layouts: 49.6 us -> 51.6 us
    unnamed x14 -> x15, waiting for transfers between devices: 76.1 us -> 76.2 us
  transfers between devices with their start and end apart: 11 -> 12, of which waited for: 10 -> 11; matrix products, arithmetic and copies ran while one was open for 13% -> 19% of each run, Pallas kernels for 0% -> 0%
where the time goes in v1:
time: 1410 us; the launch traced here: 1400 us
  waiting for transfers between devices  885 us (63%)
  matrix products  260 us (18%)
  other arithmetic  141 us (10%)
  local copies, waits for them, and re-layouts  81.4 us (6%)
  between operations  16.3 us (1%)
  blocking collectives  14.1 us (1%)
    psum x1, waiting for transfers between devices, local(): lax.psum(jnp.dot(activated, w_down, preferred_element_type=jnp.float32).a...  271 us
    all_gather x2, waiting for transfers between devices, meet_goods(): part_now = jnp.sum(jax.lax.all_gather(payload, 'tensor'), axis=0)  216 us
    psum x1, waiting for transfers between devices, local(): lax.psum(jnp.dot(context, w_out, preferred_element_type=jnp.float32).asty...  163 us
    unnamed x15, waiting for transfers between devices  76.2 us
    reduce_scatter x1, waiting for transfers between devices, local(): lax.psum_scatter(grad_w_skip.astype(jnp.bfloat16), 'dp', scatter_dimensio...  52.6 us
    unnamed x232, local copies, waits for them, and re-layouts  51.6 us
    reduce_scatter x1, waiting for transfers between devices, local(): lax.psum_scatter(grad_gamma_attn.astype(jnp.bfloat16), 'dp', scatter_dime...  42.9 us
    reduce_scatter x1, waiting for transfers between devices, local(): lax.psum_scatter(grad_gamma_ffn.astype(jnp.bfloat16), 'dp', scatter_dimen...  42.6 us
  transfers between devices with their start and end apart: 12, of which 11 were waited for; matrix products, arithmetic and copies ran while one was open for 19% of the time, Pallas kernels for 0%

profile of v1, /device:TPU:0, one launch (start us, length us, event | category | flops | bytes accessed | tf_op | source)
XLA Modules:
  0.0 1398.5 jit_solution(14919963843692695515)
XLA Ops:
  65.3 10.5 fusion.65
  78.2 10.5 fusion.59
  103.5 163.2 %all-reduce.7.cloned.1.call-done = (bf16[1152,1024]{0,1:T(8,128)(2,1)}, bf16[1152,1024]{0,1:T(8,128)(2,1)}) async-done(((bf16[1152,1024]{0,1:T(8,128)(2,1)}, bf16[1152,1024]{0,1:T(8,128)(2,1)}), (bf16[1152,1024]{0,1:T(8,128)(2,1)}, bf16[1152,1024]{0,1:T(8,128)(2,1)})) %all-reduce.7.cloned.1.call-update) | async-done | bytes 4718608 | tf_op jit(solution)/shard_map/psum | solution.py:137
  270.6 14.4 %multiply_convert_fusion.7 = (bf16[1152,1024]{1,0:T(8,128)(2,1)}, f32[1152,1024]{1,0:T(8,128)S(1)}, f32[1152,1024]{1,0:T(8,128)S(1)}) fusion(f32[1024]{0:T(1024)S(1)} %convert_element_type.432, bf16[1024,1024]{1,0:T(8,128)(2,1)S(1)} %copy-done, f32[1152,1024]{0,1:T(8,128)S(1)} %get-tuple-element.57, f32[1024]{0:T(1024)S(1)} %broadcast_add_fusion.2, ...), kind=kOutput, calls=%fused_computation.88 | convolution fusion | flops 2497314816 | bytes 18625024 | tf_op jit(solution)/shard_map/dot_general | solution.py:146
  304.7 14.2 %multiply_convert_fusion.3 = (bf16[1152,1024]{1,0:T(8,128)(2,1)}, f32[1152,1024]{1,0:T(8,128)S(1)}, f32[1152,1024]{1,0:T(8,128)S(1)}) fusion(f32[1024]{0:T(1024)S(1)} %convert_element_type.432, bf16[1024,1024]{1,0:T(8,128)(2,1)S(1)} %copy-done, f32[1152,1024]{0,1:T(8,128)S(1)} %get-tuple-element.61, f32[1024]{0:T(1024)S(1)} %get-tuple-element.140, ...), kind=kOutput, calls=%fused_computation.69 | convolution fusion | flops 2497314816 | bytes 18625024 | tf_op jit(solution)/shard_map/dot_general | solution.py:146
  342.6 118.8 %all-gather.5.cloned.1.call-done = bf16[4608,1024]{1,0:T(8,128)(2,1)} async-done(((bf16[1152,1024]{1,0:T(8,128)(2,1)}), bf16[4608,1024]{1,0:T(8,128)(2,1)}) %all-gather.5.cloned.1.call-update) | async-done | bytes 9437200 | tf_op jit(solution)/shard_map/all_gather | solution.py:13
  485.8 13.6 multiply_reduce_fusion.1
  499.4 15.0 %multiply_convert_fusion.1 = bf16[4,1152,1152]{1,2,0:T(8,128)(2,1)S(1)} fusion(f32[4,1152,1152]{1,2,0:T(8,128)} %get-tuple-element.127, f32[4,1152,1152]{1,2,0:T(8,128)} %copy-done.3, f32[4,1152]{1,0:T(4,128)S(1)} %get-tuple-element.126, f32[4,1152]{1,0:T(4,128)S(1)} %copy-done.67), kind=kLoop, calls=%fused_computation.6 | loop fusion | flops 21233664 | bytes 53121024 | tf_op jit(solution)/shard_map/convert_element_type | solution.py:188
  519.5 11.4 fusion.62
  530.9 97.0 %all-gather.7.cloned.1.call-done = bf16[4608,1024]{1,0:T(8,128)(2,1)} async-done(((bf16[1152,1024]{1,0:T(8,128)(2,1)}), bf16[4608,1024]{1,0:T(8,128)(2,1)}) %all-gather.7.cloned.1.call-update) | async-done | bytes 9437200 | tf_op jit(solution)/shard_map/all_gather | solution.py:13
  651.4 11.4 fusion.68
  662.8 13.2 multiply_reduce_fusion
  676.0 14.6 %multiply_convert_fusion = bf16[4,1152,1152]{1,2,0:T(8,128)(2,1)S(1)} fusion(f32[4,1152,1152]{1,2,0:T(8,128)} %get-tuple-element.129, f32[4,1152,1152]{1,2,0:T(8,128)} %copy-done.2, f32[4,1152]{1,0:T(4,128)S(1)} %get-tuple-element.128, f32[4,1152]{1,0:T(4,128)S(1)} %copy-done.65), kind=kLoop, calls=%fused_computation.4 | loop fusion | flops 21233664 | bytes 53121024 | tf_op jit(solution)/shard_map/convert_element_type | solution.py:188
  771.2 271.1 %all-reduce.5.cloned.1.call-done = (bf16[1152,1024]{0,1:T(8,128)(2,1)}, bf16[1152,1024]{0,1:T(8,128)(2,1)}, bf16[1152,1024]{0,1:T(8,128)(2,1)}, bf16[1152,1024]{0,1:T(8,128)(2,1)}) async-done(((bf16[1152,1024]{0,1:T(8,128)(2,1)}, bf16[1152,1024]{0,1:T(8,128)(2,1)}, bf16[1152,1024]{0,1:T(8,128)(2,1)}, bf16[1152,1024]{0,1:T(8,128)(2,1)}), (bf16[1152,1024]{0,1:T(8,128)(2,1)}, bf16[1152,1024]{0,1:T(8,128)(2,1)}, ...) | async-done | bytes 9437200 | tf_op jit(solution)/shard_map/psum | solution.py:148
  1057.1 9.5 fusion.24
  1066.6 8.2 fusion.45
  1075.1 9.8 fusion.17
  1095.1 14.1 %psum.55 = f32[1024]{0:T(1024)} all-reduce(f32[1024]{0:T(1024)S(1)} %add.242), channel_id=1, replica_groups=mesh['dp'=8,'tensor'=4] {'dp'}, use_global_device_ids=true, to_apply=%region_35.36 | all-reduce | flops 1024 | bytes 8192 | tf_op jit(solution)/shard_map/psum | solution.py:237
  1111.3 18.6 %reduce-scatter.23.cloned.1.call-done = bf16[128,1024]{1,0:T(8,128)(2,1)} async-done(((bf16[1024,1024]{1,0:T(8,128)(2,1)}), bf16[128,1024]{1,0:T(8,128)(2,1)}) %reduce-scatter.23.cloned.1.call-update) | async-done | bytes 262160 | tf_op jit(solution)/shard_map/reduce_scatter | solution.py:245
  1131.7 36.0 %reduce-scatter.27.cloned.1.call-done = bf16[128,256]{1,0:T(8,128)(2,1)} async-done(((bf16[1024,256]{1,0:T(8,128)(2,1)}), bf16[128,256]{1,0:T(8,128)(2,1)}) %reduce-scatter.27.cloned.1.call-update) | async-done | bytes 65552
  1169.3 40.0 %reduce-scatter.25.cloned.1.call-done = bf16[128,768]{1,0:T(8,128)(2,1)} async-done(((bf16[1024,768]{1,0:T(8,128)(2,1)}), bf16[128,768]{1,0:T(8,128)(2,1)}) %reduce-scatter.25.cloned.1.call-update) | async-done | bytes 196624
  1247.9 42.9 %reduce-scatter.19.cloned.1.call-done = bf16[128,1024]{1,0:T(8,128)(2,1)} async-done(((bf16[1024,1024]{1,0:T(8,128)(2,1)}), bf16[128,1024]{1,0:T(8,128)(2,1)}) %reduce-scatter.19.cloned.1.call-update) | async-done | bytes 262160 | tf_op jit(solution)/shard_map/reduce_scatter | solution.py:251
  1292.6 42.6 %reduce-scatter.21.cloned.1.call-done = bf16[128,1024]{1,0:T(8,128)(2,1)} async-done(((bf16[1024,1024]{1,0:T(8,128)(2,1)}), bf16[128,1024]{1,0:T(8,128)(2,1)}) %reduce-scatter.21.cloned.1.call-update) | async-done | bytes 262160 | tf_op jit(solution)/shard_map/reduce_scatter | solution.py:254
  1337.0 52.6 %reduce-scatter.17.cloned.1.call-done = bf16[256,1024]{1,0:T(8,128)(2,1)} async-done(((bf16[2048,1024]{1,0:T(8,128)(2,1)}), bf16[256,1024]{1,0:T(8,128)(2,1)}) %reduce-scatter.17.cloned.1.call-update) | async-done | bytes 524304 | tf_op jit(solution)/shard_map/reduce_scatter | solution.py:260
  (385 shorter events, 329.0 us)
Async XLA Ops:
  7.2 263.4 %copy-start = (bf16[1024,1024]{1,0:T(8,128)(2,1)S(1)}, bf16[1024,1024]{1,0:T(8,128)(2,1)}, u32[]{:S(2)}) copy-start(bf16[1024,1024]{1,0:T(8,128)(2,1)} %param.25) | copy-start | bytes 6291460
  7.2 259.5 %all-reduce.7.cloned.1.call-start = ((), (), s32[]{:S(2)}) async-start(), calls=%async_computation.19 | async-start | bytes 9437184 | tf_op jit(solution)/shard_map/psum | solution.py:137
  26.4 51.8 %copy-start.28 = (bf16[1,1152,256]{1,2,0:T(8,128)(2,1)}, bf16[1,1152,256]{1,2,0:T(8,128)(2,1)S(1)}, u32[]{:S(2)}) copy-start(bf16[1,1152,256]{1,2,0:T(8,128)(2,1)S(1)} %slice.289) | copy-start | bytes 1769476
  38.6 26.6 %copy-start.26 = (bf16[1,1152,256]{1,2,0:T(8,128)(2,1)}, bf16[1,1152,256]{1,2,0:T(8,128)(2,1)S(1)}, u32[]{:S(2)}) copy-start(bf16[1,1152,256]{1,2,0:T(8,128)(2,1)S(1)} %slice.288) | copy-start | bytes 1769476
  91.8 369.6 %all-gather.5.cloned.1.call-start = ((), (), s32[]{:S(2)}) async-start(), calls=%async_computation.13 | async-start | bytes 11796480 | tf_op jit(solution)/shard_map/all_gather | solution.py:13
  270.5 14.5 %copy-start.5 = (f32[1152,1024]{0,1:T(8,128)}, f32[1152,1024]{0,1:T(8,128)S(1)}, u32[]{:S(2)}) copy-start(f32[1152,1024]{0,1:T(8,128)S(1)} %get-tuple-element.57) | copy-start | bytes 14155780
  270.6 14.5 %copy-start.14 = (bf16[1,1,1152,1024]{2,3,1,0:T(8,128)(2,1)S(1)}, bf16[1,1,1152,1024]{2,3,1,0:T(8,128)(2,1)}, u32[]{:S(2)}) copy-start(bf16[1,1,1152,1024]{2,3,1,0:T(8,128)(2,1)} %copy.126) | copy-start | bytes 7077892
  270.6 14.5 %copy-start.100 = (bf16[1024,1024]{1,0:T(8,128)(2,1)S(1)}, bf16[1024,1024]{1,0:T(8,128)(2,1)}, u32[]{:S(2)}) copy-start(bf16[1024,1024]{1,0:T(8,128)(2,1)} %param.27) | copy-start | bytes 6291460
  295.5 332.4 %all-gather.7.cloned.1.call-start = ((), (), s32[]{:S(2)}) async-start(), calls=%async_computation.14 | async-start | bytes 11796480 | tf_op jit(solution)/shard_map/all_gather | solution.py:13
  304.7 14.3 %copy-start.4 = (f32[1152,1024]{0,1:T(8,128)}, f32[1152,1024]{0,1:T(8,128)S(1)}, u32[]{:S(2)}) copy-start(f32[1152,1024]{0,1:T(8,128)S(1)} %get-tuple-element.61) | copy-start | bytes 14155780
  336.4 705.9 %all-reduce.5.cloned.1.call-start = ((), (), s32[]{:S(2)}) async-start(), calls=%async_computation.18 | async-start | bytes 18874368 | tf_op jit(solution)/shard_map/psum | solution.py:148
  499.3 15.0 %copy-start.43 = (bf16[1152,4,32]{0,2,1:T(8,128)(2,1)S(1)}, bf16[1152,4,32]{0,2,1:T(8,128)(2,1)}, u32[]{:S(2)}) copy-start(bf16[1152,4,32]{0,2,1:T(8,128)(2,1)} %copy-done.42) | copy-start | bytes 884740
  499.4 15.0 %copy-start.45 = (bf16[1152,4,32]{0,2,1:T(8,128)(2,1)S(1)}, bf16[1152,4,32]{0,2,1:T(8,128)(2,1)}, u32[]{:S(2)}) copy-start(bf16[1152,4,32]{0,2,1:T(8,128)(2,1)} %copy-done.44) | copy-start | bytes 884740
  676.0 14.6 %copy-start.35 = (bf16[1152,4,32]{0,2,1:T(8,128)(2,1)S(1)}, bf16[1152,4,32]{0,2,1:T(8,128)(2,1)}, u32[]{:S(2)}) copy-start(bf16[1152,4,32]{0,2,1:T(8,128)(2,1)} %copy-done.34) | copy-start | bytes 884740
  676.0 14.6 %copy-start.37 = (bf16[1152,4,32]{0,2,1:T(8,128)(2,1)S(1)}, bf16[1152,4,32]{0,2,1:T(8,128)(2,1)}, u32[]{:S(2)}) copy-start(bf16[1152,4,32]{0,2,1:T(8,128)(2,1)} %copy-done.36) | copy-start | bytes 884740
  719.3 389.9 %reduce-scatter.29.cloned.1.call-start = ((), (), s32[]{:S(2)}) async-start(), calls=%async_computation.17 | async-start | bytes 2359296
  731.1 398.8 %reduce-scatter.23.cloned.1.call-start = ((), (), s32[]{:S(2)}) async-start(), calls=%async_computation.12 | async-start | bytes 2359296 | tf_op jit(solution)/shard_map/reduce_scatter | solution.py:245
  743.7 424.0 %reduce-scatter.27.cloned.1.call-start = ((), (), s32[]{:S(2)}) async-start(), calls=%async_computation.16 | async-start | bytes 589824
  751.3 458.1 %reduce-scatter.25.cloned.1.call-start = ((), (), s32[]{:S(2)}) async-start(), calls=%async_computation.15 | async-start | bytes 1769472
  769.7 476.8 %reduce-scatter.15.cloned.1.call-start = ((), (), s32[]{:S(2)}) async-start(), calls=%async_computation.8 | async-start | bytes 147456 | tf_op jit(solution)/shard_map/reduce_scatter | solution.py:257
  1053.0 237.8 %reduce-scatter.19.cloned.1.call-start = ((), (), s32[]{:S(2)}) async-start(), calls=%async_computation.10 | async-start | bytes 2359296 | tf_op jit(solution)/shard_map/reduce_scatter | solution.py:251
  1055.8 279.4 %reduce-scatter.21.cloned.1.call-start = ((), (), s32[]{:S(2)}) async-start(), calls=%async_computation.11 | async-start | bytes 2359296 | tf_op jit(solution)/shard_map/reduce_scatter | solution.py:254
  1074.8 314.8 %reduce-scatter.17.cloned.1.call-start = ((), (), s32[]{:S(2)}) async-start(), calls=%async_computation.9 | async-start | bytes 4718592 | tf_op jit(solution)/shard_map/reduce_scatter | solution.py:260
  1242.2 149.0 %copy-start.1 = (bf16[1024,1024]{1,0:T(8,128)(2,1)S(1)}, bf16[1024,1024]{1,0:T(8,128)(2,1)}, u32[]{:S(2)}) copy-start(bf16[1024,1024]{1,0:T(8,128)(2,1)} %param.25) | copy-start | bytes 6291460
  (98 other events, 591.7 us)
Sparse Core Ops, SparseCore 0:
  91.9 174.7 all-reduce.6
  295.6 165.7 all-gather.4
  463.0 164.9 all-gather.6
  719.4 322.8 all-reduce.4
  1045.5 40.0 reduce-scatter.28
  1088.7 41.1 reduce-scatter.22
  1133.5 34.1 reduce-scatter.26
  1171.0 38.3 reduce-scatter.24
  1212.9 33.5 reduce-scatter.14
  1249.7 41.0 reduce-scatter.18
  1294.1 41.0 reduce-scatter.20
  1338.4 51.1 reduce-scatter.16
